TPU v7x, 32 devices: a whole 2x2x4 slice. The times are simulated.
32 devices in a mesh: ctx: 8 (over z, x), head: 4 (over y, core).
Axes of the slice: x: 2, y: 2, z: 4, core: 2. Of those that a mesh axis runs over, the one named last changes fastest.
Arguments:
- qkv: bfloat16 [4096, 12288], P(('ctx', 'head')), may hold values from -26 to 26
- grad_out: bfloat16 [4096, 4096], P(('ctx', 'head')), may hold values from -6 to 6
- key_lists: int32 [32, 4], P('ctx'), may hold values from 0 to 31, as said below
- live_counts: int32 [32], P('ctx'), may hold values from 1 to 4
Outputs:
- grad_qkv: bfloat16 [4096, 12288], P(('ctx', 'head'))
Inputs may be any that keep to these rules, and one draw needn't show every extreme that they name: `key_lists`: each entry names a block whose index of ctx is within 2 of its query block's and which is not within one block of its query block; the 4 entries of a row differ. Over all 4 entries of all rows (live or not) of one index of ctx, the blocks named on any other index of ctx are at most 2 of its blocks, and this is reached.
All inputs are finite; a program needn't handle non-finite values.
Results may differ from a plain program's by a relative error of at most 0.008.
Values may be sent and summed in bfloat16 or wider, within the bound.
A program may use at most 192 MiB of HBM per device.

v0:
```python
import jax
import jax.numpy as jnp
from jax import lax
from jax.sharding import PartitionSpec as P

HD = 128
BLK = 128
SEARCHER_TILES = 4
DRAWN_TARGET_SET = 4
SPAN = 2
NAMED_TILE_LIMIT = 2


def extended_2(cells, sides, width):
    for axis, dim in sides:
        count = lax.axis_size(axis)
        ends = count - 1
        head = lax.slice_in_dim(cells, 0, width, axis=dim)
        tail = lax.slice_in_dim(cells, cells.shape[dim] - width, cells.shape[dim], axis=dim)
        cells = jnp.concatenate(
            [
                lax.ppermute(tail, axis, [(i, (i + 1) % count) for i in range(ends)]),
                cells,
                lax.ppermute(head, axis, [((i + 1) % count, i) for i in range(ends)]),
            ],
            axis=dim,
        )
    return cells


def from_behind(value, axis, steps):
    count = lax.axis_size(axis)
    initial, last = (max(0, -steps), min(count, count - steps))
    return lax.ppermute(value, axis, [(source, source + steps) for source in range(initial, last)])


def block_grads(query_part, grad_part, key_part, value_part, usable):
    scaling = HD ** (-0.5)
    tile_merits = (
        jnp.einsum("qhd,nkhd->hqnk", query_part, key_part, preferred_element_type=jnp.float32)
        * scaling
    )
    weight = usable.astype(jnp.float32)[None, None, :, None]
    masked = jnp.where(weight > 0.0, tile_merits, -1e30)
    highest = jnp.max(masked, axis=(2, 3), keepdims=True)
    powers = jnp.exp(masked - highest) * weight
    soft_weights = powers / jnp.sum(powers, axis=(2, 3), keepdims=True)
    grad_soft = jnp.einsum(
        "qhd,nkhd->hqnk", grad_part, value_part, preferred_element_type=jnp.float32
    )
    row_delta = jnp.sum(soft_weights * grad_soft, axis=(2, 3), keepdims=True)
    grad_scores = soft_weights * (grad_soft - row_delta)
    soft_low = soft_weights.astype(jnp.bfloat16)
    scores_low = grad_scores.astype(jnp.bfloat16)
    grad_values = jnp.einsum(
        "hqnk,qhd->nkhd", soft_low, grad_part, preferred_element_type=jnp.float32
    )
    grad_keys = (
        jnp.einsum("hqnk,qhd->nkhd", scores_low, query_part, preferred_element_type=jnp.float32)
        * scaling
    )
    grad_query = (
        jnp.einsum("hqnk,nkhd->qhd", scores_low, key_part, preferred_element_type=jnp.float32)
        * scaling
    )
    return (grad_query, jnp.stack([grad_keys, grad_values], axis=3))


def needed_blocks(list_rows, owner_shard):
    targets = owner_shard * SEARCHER_TILES + jnp.arange(SEARCHER_TILES, dtype=jnp.int32)
    matches = list_rows[:, :, None] == targets[None, None, :]
    return jnp.any(matches, axis=(0, 1))


def slot_numbers(needed):
    block_order = jnp.arange(SEARCHER_TILES, dtype=jnp.int32)
    earlier = block_order[None, :] < block_order[:, None]
    return jnp.sum(jnp.where(earlier & needed[None, :], 1, 0), axis=1).astype(jnp.int32)


def select_table(needed):
    slot_of = slot_numbers(needed)
    slot_range = jnp.arange(NAMED_TILE_LIMIT, dtype=jnp.int32)
    return (needed[None, :] & (slot_of[None, :] == slot_range[:, None])).astype(jnp.float32)


def shards(qkv, grad_out, key_lists, live_counts):
    merged, grad_rows = (
        lax.all_to_all(qkv, "head", split_axis=1, concat_axis=0, tiled=True),
        lax.all_to_all(grad_out, "head", split_axis=1, concat_axis=0, tiled=True),
    )
    row_count = merged.shape[0]
    head_count = grad_rows.shape[1] // HD
    pair_width = head_count * 2 * HD
    per_head = merged.reshape(row_count, head_count, 3, HD)
    query_rows = per_head[:, :, 0]
    pair_rows = per_head[:, :, 1:].reshape(row_count, pair_width)
    shard_index = lax.axis_index("ctx")
    total_blocks = SEARCHER_TILES * lax.axis_size("ctx")
    local_ids = shard_index * SEARCHER_TILES + jnp.arange(SEARCHER_TILES, dtype=jnp.int32)
    window = local_ids[:, None] - 1 + jnp.arange(3, dtype=jnp.int32)[None, :]
    window_ok = (window >= 0) & (window < total_blocks)
    listed_ok = jnp.arange(DRAWN_TARGET_SET, dtype=jnp.int32)[None, :] < live_counts[:, None]
    usable = jnp.concatenate([window_ok, listed_ok], axis=1)
    offsets = [offset for offset in range(-SPAN, SPAN + 1) if offset != 0]
    owner_tables = []
    rims = extended_2(pair_rows, (("ctx", 0),), BLK)
    pieces = [rims]
    rank_list = []
    own_blocks = pair_rows.reshape(SEARCHER_TILES, BLK, pair_width)
    for offset in offsets:
        wanted = needed_blocks(key_lists, shard_index + offset)
        rank_list.append(slot_numbers(wanted))
        theirs = from_behind(key_lists, "ctx", offset)
        owner_table = select_table(needed_blocks(theirs, shard_index))
        owner_tables.append(owner_table)
        outgoing = jnp.einsum(
            "st,tbf->sbf",
            owner_table.astype(jnp.bfloat16),
            own_blocks,
            preferred_element_type=jnp.float32,
        )
        outgoing = outgoing.astype(jnp.bfloat16).reshape(NAMED_TILE_LIMIT * BLK, pair_width)
        pieces.append(from_behind(outgoing, "ctx", -offset))
    extended = jnp.concatenate(pieces, axis=0)
    rank_table = jnp.stack(rank_list)
    gap_shard = key_lists // SEARCHER_TILES - shard_index
    block_in = key_lists % SEARCHER_TILES
    side_of = jnp.where(gap_shard < 0, gap_shard + SPAN, gap_shard + SPAN - 1)
    side_hit = side_of[:, :, None] == jnp.arange(2 * SPAN, dtype=jnp.int32)[None, None, :]
    block_hit = block_in[:, :, None] == jnp.arange(SEARCHER_TILES, dtype=jnp.int32)[None, None, :]
    rank_here = jnp.sum(
        jnp.where(side_hit[:, :, :, None] & block_hit[:, :, None, :], rank_table[None, None], 0),
        axis=(2, 3),
    )
    far_place = SEARCHER_TILES + 2 + side_of * NAMED_TILE_LIMIT + rank_here
    listed_place = jnp.where(gap_shard == 0, 1 + block_in, far_place)
    window_place = jnp.clip(window - shard_index * SEARCHER_TILES + 1, 0, SEARCHER_TILES + 1)
    places = jnp.concatenate([window_place, listed_place], axis=1)
    block_count = extended.shape[0] // BLK
    tile_ordinals = extended.reshape(block_count, BLK, head_count, 2, HD)
    query_blocks = query_rows.reshape(SEARCHER_TILES, BLK, head_count, HD)
    grad_blocks = grad_rows.reshape(SEARCHER_TILES, BLK, head_count, HD)

    def step(carry, inputs):
        query_part, grad_part, block_places, block_ok = inputs
        chosen = tile_ordinals[block_places]
        grad_query, grad_pairs = block_grads(
            query_part, grad_part, chosen[:, :, :, 0], chosen[:, :, :, 1], block_ok
        )
        return (carry, (grad_query, grad_pairs))

    carry_zero = jnp.zeros((), jnp.float32)
    carry_zero, outputs = lax.scan(step, carry_zero, (query_blocks, grad_blocks, places, usable))
    grad_query, pair_terms = outputs
    slot_total = pair_terms.shape[0] * pair_terms.shape[1]
    flat_terms = pair_terms.reshape(slot_total, BLK * pair_width)
    place_flat = places.reshape(slot_total)
    owner_hits = (place_flat[None, :] == jnp.arange(block_count, dtype=jnp.int32)[:, None]).astype(
        jnp.float32
    )
    totals = jnp.dot(
        owner_hits, flat_terms, precision=lax.Precision.HIGHEST, preferred_element_type=jnp.float32
    )
    totals = totals.reshape(block_count, BLK, pair_width)
    own_grads = totals[1 : SEARCHER_TILES + 1]
    for direction in (-1, 1):
        rim_rows = totals[0] if direction == -1 else totals[SEARCHER_TILES + 1]
        arrived = from_behind(rim_rows.astype(jnp.bfloat16), "ctx", direction).astype(
            rim_rows.dtype
        )
        target_block = SEARCHER_TILES - 1 if direction == -1 else 0
        own_grads = own_grads.at[target_block].add(arrived)
    for side_index, offset in enumerate(offsets):
        first_slot = SEARCHER_TILES + 2 + side_index * NAMED_TILE_LIMIT
        arrived = from_behind(totals[first_slot : first_slot + NAMED_TILE_LIMIT], "ctx", offset)
        own_grads = own_grads + jnp.einsum(
            "st,sbf->tbf", owner_tables[side_index], arrived, precision=lax.Precision.HIGHEST
        )
    own_grads = own_grads.reshape(SEARCHER_TILES, BLK, head_count, 2, HD)
    joined = jnp.concatenate([grad_query[:, :, :, None, :], own_grads], axis=3)
    joined = joined.astype(jnp.bfloat16).reshape(row_count, head_count * 3 * HD)
    return lax.all_to_all(joined, "head", split_axis=0, concat_axis=1, tiled=True)


def solution(mesh):
    placed = (P(("ctx", "head"), None), P(("ctx", "head"), None), P("ctx", None), P("ctx"))
    return jax.shard_map(
        shards, mesh=mesh, in_specs=placed, out_specs=P(("ctx", "head"), None), check_vma=False
    )
```

profile of v0, /device:TPU:0, one launch (start us, length us, event | category | flops | bytes accessed | tf_op | source)
XLA Modules:
  0.0 669.7 jit_solution(15242273154368790769)
XLA Ops:
  0.0 4.9 collective-permute-start.8
  5.0 3.4 collective-permute-start.6
  11.0 4.6 copy.138
  15.6 3.8 all-to-all-start
  19.6 2.3 copy.153
  24.3 32.0 %all-to-all-done = bf16[128,4,3072]{0,2,1:T(8,128)(2,1)S(1)} async-done(((bf16[128,4,3072]{0,2,1:T(8,128)(2,1)}), bf16[128,4,3072]{0,2,1:T(8,128)(2,1)S(1)}, u32[]{:S(2)}, u32[]{:S(2)}) %all-to-all-start) | async-done | bytes 3145760 | tf_op jit(solution)/shard_map/all_to_all | solution.py:89
  56.3 4.2 all-to-all-start.1
  60.6 15.6 %copy.139 = bf16[4,128,3072]{1,0,2:T(4,128)(2,1)} copy(bf16[4,128,3072]{1,2,0:T(8,128)(2,1)S(1)} %bitcast.205) | data formatting | bytes 6291456 | tf_op jit(solution)/shard_map/all_to_all | solution.py:89
  76.1 4.0 reshape.223
  86.0 5.5 collective-permute-start
  91.5 2.1 reshape.260
  93.5 2.5 copy.151
  98.3 4.6 copy.143
  105.6 7.1 %collective-permute-start.3 = (bf16[256,2048]{1,0:T(8,128)(2,1)}, bf16[256,2048]{1,0:T(8,128)(2,1)}, u32[]{:S(2)}, u32[]{:S(2)}) collective-permute-start(bf16[256,2048]{1,0:T(8,128)(2,1)} %bitcast.34), channel_id=1, source_target_pairs={{0,8},{4,12},{8,16},{12,20},{16,24},{20,28},{1,9},{5,13},{9,17},{1... | collective-permute-start | bytes 3145736 | tf_op jit(solution)/shard_map/ppermute | solution.py:34
  115.3 4.1 collective-permute-start.5
  123.3 3.0 convolution_convert_fusion
  135.7 2.3 constant_dynamic-update-slice_fusion.3
  138.0 25.6 %collective-permute-done.5 = bf16[256,2048]{1,0:T(8,128)(2,1)} collective-permute-done((bf16[256,2048]{1,0:T(8,128)(2,1)}, bf16[256,2048]{1,0:T(8,128)(2,1)}, u32[]{:S(2)}, u32[]{:S(2)}) %collective-permute-start.5) | collective-permute-done | bytes 1048608 | tf_op jit(solution)/shard_map/ppermute | solution.py:34
  163.6 2.3 constant_dynamic-update-slice_fusion.2
  165.9 2.4 constant_dynamic-update-slice_fusion.1
  168.3 3.1 collective-permute-done.9
  172.4 12.6 %reshape.229 = bf16[14,128,8,2,128]{4,3,2,1,0:T(2,128)(2,1)} reshape(bf16[1792,2048]{1,0:T(8,128)(2,1)} %constant_dynamic-update-slice_fusion) | data formatting | bytes 14680064 | tf_op jit(solution)/shard_map/reshape | solution.py:141
  185.0 7.5 %copy.154 = bf16[14,128,8,2,128]{4,2,3,1,0:T(8,128)(2,1)} copy(bf16[14,128,8,2,128]{4,3,2,1,0:T(2,128)(2,1)} %reshape.229) | data formatting | bytes 14680064 | tf_op jit(solution)/shard_map/while | solution.py:154
  192.5 143.2 %while.14 = (s32[]{:T(128)}, bf16[4,128,8,128]{1,3,2,0:T(8,128)(2,1)S(1)}, f32[4,7,128,8,2,128]{5,4,3,2,1,0:T(2,128)}, s32[4,7]{1,0:T(4,128)S(1)}, bf16[14,128,8...) while((s32[]{:T(128)}, ...), condition=%wide.region_21.22_spmd, body=%wide.region_17.21_spmd.sunk | while | flops 1203894272 | bytes 104907184 | solution.py:154
  192.7 6.1 gather_fusion
  198.7 2.3 fusion.126
  210.0 2.1 convolution_bitcast_fusion.2
  212.7 3.9 maximum_bitcast_fusion.2
  216.6 11.7 %copy_dynamic-update-slice_fusion.2 = f32[4,7,128,8,2,128]{5,4,3,2,1,0:T(2,128)} fusion(f32[4,7,128,8,2,128]{5,4,3,2,1,0:T(2,128)} %get-tuple-element.224, s32[]{:T(128)S(6)} %copy.226, f32[1,7,128,8,2,128]{5,2,1,3,4,0:T(8,128)} %maximum_bitcast_fusion.2), kind=kLoop, calls=%fused_computation.2.clone.1 | loop fusion | bytes 14680068 | tf_op jit(solution)/shard_map/while/body/jit(dynamic_update_index_in_dim)/dynamic_update_slice | solution.py:154
  228.3 6.1 gather_fusion
  234.3 2.3 fusion.126
  245.6 2.1 convolution_bitcast_fusion.2
  248.3 3.9 maximum_bitcast_fusion.2
  252.2 11.8 %copy_dynamic-update-slice_fusion.2 = f32[4,7,128,8,2,128]{5,4,3,2,1,0:T(2,128)} fusion(f32[4,7,128,8,2,128]{5,4,3,2,1,0:T(2,128)} %get-tuple-element.224, s32[]{:T(128)S(6)} %copy.226, f32[1,7,128,8,2,128]{5,2,1,3,4,0:T(8,128)} %maximum_bitcast_fusion.2), kind=kLoop, calls=%fused_computation.2.clone.1 | loop fusion | bytes 14680068 | tf_op jit(solution)/shard_map/while/body/jit(dynamic_update_index_in_dim)/dynamic_update_slice | solution.py:154
  264.0 6.1 gather_fusion
  270.1 2.3 fusion.126
  281.3 2.1 convolution_bitcast_fusion.2
  284.0 3.9 maximum_bitcast_fusion.2
  287.9 11.8 %copy_dynamic-update-slice_fusion.2 = f32[4,7,128,8,2,128]{5,4,3,2,1,0:T(2,128)} fusion(f32[4,7,128,8,2,128]{5,4,3,2,1,0:T(2,128)} %get-tuple-element.224, s32[]{:T(128)S(6)} %copy.226, f32[1,7,128,8,2,128]{5,2,1,3,4,0:T(8,128)} %maximum_bitcast_fusion.2), kind=kLoop, calls=%fused_computation.2.clone.1 | loop fusion | bytes 14680068 | tf_op jit(solution)/shard_map/while/body/jit(dynamic_update_index_in_dim)/dynamic_update_slice | solution.py:154
  299.7 6.1 gather_fusion
  305.8 2.3 fusion.126
  317.0 2.1 convolution_bitcast_fusion.2
  319.7 3.9 maximum_bitcast_fusion.2
  323.7 11.7 %copy_dynamic-update-slice_fusion.2 = f32[4,7,128,8,2,128]{5,4,3,2,1,0:T(2,128)} fusion(f32[4,7,128,8,2,128]{5,4,3,2,1,0:T(2,128)} %get-tuple-element.224, s32[]{:T(128)S(6)} %copy.226, f32[1,7,128,8,2,128]{5,2,1,3,4,0:T(8,128)} %maximum_bitcast_fusion.2), kind=kLoop, calls=%fused_computation.2.clone.1 | loop fusion | bytes 14680068 | tf_op jit(solution)/shard_map/while/body/jit(dynamic_update_index_in_dim)/dynamic_update_slice | solution.py:154
  335.7 51.0 %reshape.231 = f32[28,262144]{1,0:T(8,128)} reshape(f32[4,7,128,8,2,128]{5,4,3,2,1,0:T(2,128)} %get-tuple-element.73) | data formatting | bytes 58720256 | tf_op jit(solution)/shard_map/reshape | solution.py:157
  386.7 25.8 %fusion.84 = (bf16[14,262144]{1,0:T(8,128)(2,1)}, f32[14,262144]{1,0:T(8,128)}) fusion(f32[28,262144]{1,0:T(8,128)} %reshape.231, s32[28]{0:T(128)S(1)} %copy-done.27), kind=kOutput, calls=%fused_computation.152 | convolution fusion | flops 1236795776 | bytes 51380336 | tf_op jit(solution)/shard_map/dot_general | solution.py:162
  412.4 15.1 %fusion.82 = (f32[2,262144]{1,0:T(2,128)}, f32[2,262144]{1,0:T(2,128)}, f32[2,262144]{1,0:T(2,128)}, f32[2,262144]{1,0:T(2,128)}) fusion(f32[14,262144]{1,0:T(8,128)} %get-tuple-element.145), kind=kLoop, calls=%fused_computation.150 | loop fusion | bytes 16777216 | tf_op jit(solution)/shard_map/slice | solution.py:176
  427.5 2.7 collective-permute-start.14
  431.5 13.9 %slice_reduce_fusion = (bf16[262144]{0:T(1024)(128)(2,1)S(1)}, bf16[262144]{0:T(1024)(128)(2,1)S(1)}) fusion(bf16[14,262144]{1,0:T(8,128)(2,1)} %get-tuple-element.144), kind=kLoop, calls=%fused_computation.47 | loop fusion | bytes 2097152 | tf_op jit(solution)/shard_map/slice | solution.py:168
  447.9 7.5 %collective-permute-start.11 = (bf16[128,2048]{1,0:T(8,128)(2,1)}, bf16[128,2048]{1,0:T(8,128)(2,1)}, u32[]{:S(2)}, u32[]{:S(2)}) collective-permute-start(bf16[128,2048]{1,0:T(8,128)(2,1)} %convert_element_type.88), channel_id=1, source_target_pairs={{0,4},{4,8},{8,12},{12,16},{16,20},{20,24},{24,28},{1,5},{5,9},{9,... | collective-permute-start | bytes 1572872 | tf_op jit(solution)/shard_map/ppermute | solution.py:34
  456.7 13.2 %slice_reduce_fusion.2 = f32[262144]{0:T(1024)S(1)} fusion(f32[14,262144]{1,0:T(8,128)} %get-tuple-element.145), kind=kLoop, calls=%fused_computation.50 | loop fusion | bytes 2097152 | tf_op jit(solution)/shard_map/slice.64
  469.9 5.2 slice.140
  475.3 16.0 %collective-permute-done.10 = bf16[128,2048]{1,0:T(8,128)(2,1)S(1)} collective-permute-done((bf16[128,2048]{1,0:T(8,128)(2,1)S(1)}, bf16[128,2048]{1,0:T(8,128)(2,1)S(1)}, u32[]{:S(2)}, u32[]{:S(2)}) %collective-permute-start.10) | collective-permute-done | bytes 524320 | tf_op jit(solution)/shard_map/ppermute | solution.py:34
  492.1 57.7 %collective-permute-start.15 = (f32[2,128,2048]{2,0,1:T(2,128)}, f32[2,128,2048]{2,0,1:T(2,128)S(1)}, u32[]{:S(2)}, u32[]{:S(2)}) collective-permute-start(f32[2,128,2048]{2,0,1:T(2,128)} %bitcast.214), channel_id=1, source_target_pairs={{0,8},{4,12},{8,16},{12,20},{16,24},{20,28},{1,9},{5,13},{9,17},{1... | collective-permute-start | bytes 6291464 | tf_op jit(solution)/shard_map/ppermute | solution.py:34
  551.7 19.7 %scatter-add.6 = f32[4,128,2048]{2,0,1:T(4,128)} dynamic-update-slice(f32[4,128,2048]{2,0,1:T(4,128)} %bitcast.203, f32[1,128,2048]{2,0,1:T(1,128)S(1)} %add.185, s32[]{:T(128)} %constant.137.clone.1, s32[]{:T(128)} %constant.129.clone.1, s32[]{:T(128)} %constant.129.clone.1) | dynamic-update-slice | bytes 2097156 | tf_op jit(solution)/shard_map/scatter-add | solution.py:173
  572.6 2.9 slice_add_fusion
  575.5 19.5 %scatter-add.9 = f32[4,128,2048]{2,0,1:T(4,128)} dynamic-update-slice(f32[4,128,2048]{2,0,1:T(4,128)} %scatter-add.6, f32[1,128,2048]{2,0,1:T(1,128)S(1)} %slice_add_fusion, s32[]{:T(128)} %constant.129.clone.1, s32[]{:T(128)} %constant.129.clone.1, s32[]{:T(128)} %constant.129.clone.1) | dynamic-update-slice | bytes 2097156 | tf_op jit(solution)/shard_map/scatter-add | solution.py:173
  595.0 6.4 fusion.54
  601.4 6.4 fusion.56
  607.9 6.5 fusion.58
  614.4 8.8 %add_convert_fusion = bf16[4,128,2048]{2,0,1:T(4,128)(2,1)} fusion(f32[4,128,2048]{2,0,1:T(4,128)S(1)} %fusion.54, f32[4,128,2048]{2,0,1:T(4,128)S(1)} %fusion.56, f32[4,128,2048]{2,0,1:T(4,128)S(1)} %copy-done, f32[4,128,2048]{2,0,1:T(4,128)S(1)} %fusion.58, f32[2,128,2048]{2,0,1:T(2,128)S(1)} %collective-permute-done.15, pred[4]{0:T(512)(128)(4,1)S(1)} %copy-done.12, ...), kind=kOutput, calls=%fused_computation.41 | convolution fusion | flops 30408720 | bytes 20971540 | tf_op jit(solution)/shard_map/st,sbf->tbf/dot_general | solution.py:177
  623.2 3.5 copy.183
  627.1 39.4 %all_to_all.48 = bf16[4,128,3072]{1,2,0:T(8,128)(2,1)S(1)} all-to-all(bf16[4,128,3072]{1,2,0:T(8,128)(2,1)S(1)} %bitcast.207), channel_id=1, replica_groups=mesh['ctx'=8,'head'=4] {'head'}, dimensions={0} | all-to-all | bytes 6291456 | tf_op jit(solution)/shard_map/all_to_all | solution.py:183
  666.5 2.8 copy.164
  (186 shorter events, 80.0 us)
Async XLA Ops:
  0.0 23.8 %collective-permute-start.8 = (s32[4,4]{1,0:T(4,128)}, s32[4,4]{1,0:T(4,128)S(1)}, u32[]{:S(2)}, u32[]{:S(2)}) collective-permute-start(s32[4,4]{1,0:T(4,128)} %param.12), channel_id=1, source_target_pairs={{0,8},{4,12},{8,16},{12,20},{16,24},{20,28},{1,9},{5,13},{9,17},{1... | collective-permute-start | bytes 200 | tf_op jit(solution)/shard_map/ppermute | solution.py:34
  5.0 18.9 %collective-permute-start.6 = (s32[4,4]{1,0:T(4,128)}, s32[4,4]{1,0:T(4,128)S(1)}, u32[]{:S(2)}, u32[]{:S(2)}) collective-permute-start(s32[4,4]{1,0:T(4,128)} %param.12), channel_id=1, source_target_pairs={{0,4},{4,8},{8,12},{12,16},{16,20},{20,24},{24,28},{1,5},{5,9},{9,... | collective-permute-start | bytes 200 | tf_op jit(solution)/shard_map/ppermute | solution.py:34
  8.4 15.5 %collective-permute-start.2 = (s32[4,4]{1,0:T(4,128)}, s32[4,4]{1,0:T(4,128)S(1)}, u32[]{:S(2)}, u32[]{:S(2)}) collective-permute-start(s32[4,4]{1,0:T(4,128)} %param.12), channel_id=1, source_target_pairs={{8,0},{12,4},{16,8},{20,12},{24,16},{28,20},{9,1},{13,5},{17,9},{2... | collective-permute-start | bytes 200 | tf_op jit(solution)/shard_map/ppermute | solution.py:34
  9.7 14.2 %collective-permute-start.4 = (s32[4,4]{1,0:T(4,128)}, s32[4,4]{1,0:T(4,128)S(1)}, u32[]{:S(2)}, u32[]{:S(2)}) collective-permute-start(s32[4,4]{1,0:T(4,128)} %param.12), channel_id=1, source_target_pairs={{4,0},{8,4},{12,8},{16,12},{20,16},{24,20},{28,24},{5,1},{9,5},{13... | collective-permute-start | bytes 200 | tf_op jit(solution)/shard_map/ppermute | solution.py:34
  15.6 3.9 copy-start.28
  15.6 6.5 copy-start.10
  15.6 40.7 %all-to-all-start = ((bf16[128,4,3072]{0,2,1:T(8,128)(2,1)}), bf16[128,4,3072]{0,2,1:T(8,128)(2,1)S(1)}, u32[]{:S(2)}, u32[]{:S(2)}) async-start(bf16[128,4,3072]{0,2,1:T(8,128)(2,1)} %bitcast.206), calls=%async_computation | async-start | bytes 6291456 | tf_op jit(solution)/shard_map/all_to_all | solution.py:89
  23.9 79.0 %copy-start.13 = (pred[4]{0:T(512)(128)(4,1)}, pred[4]{0:T(512)(128)(4,1)S(1)}, u32[]{:S(2)}) copy-start(pred[4]{0:T(512)(128)(4,1)S(1)} %get-tuple-element.114) | copy-start | bytes 16
  23.9 88.8 %copy-start.15 = (pred[4]{0:T(512)(128)(4,1)}, pred[4]{0:T(512)(128)(4,1)S(1)}, u32[]{:S(2)}) copy-start(pred[4]{0:T(512)(128)(4,1)S(1)} %get-tuple-element.115) | copy-start | bytes 16
  24.0 95.5 %copy-start.17 = (pred[4]{0:T(512)(128)(4,1)}, pred[4]{0:T(512)(128)(4,1)S(1)}, u32[]{:S(2)}) copy-start(pred[4]{0:T(512)(128)(4,1)S(1)} %get-tuple-element.113) | copy-start | bytes 16
  24.0 99.4 %copy-start.11 = (pred[4]{0:T(512)(128)(4,1)}, pred[4]{0:T(512)(128)(4,1)S(1)}, u32[]{:S(2)}) copy-start(pred[4]{0:T(512)(128)(4,1)S(1)} %get-tuple-element.112) | copy-start | bytes 16
  24.1 78.9 %copy-start.21 = (s32[4]{0:T(128)}, s32[4]{0:T(128)S(1)}, u32[]{:S(2)}) copy-start(s32[4]{0:T(128)S(1)} %get-tuple-element.155) | copy-start | bytes 52
  24.1 88.6 %copy-start.23 = (s32[4]{0:T(128)}, s32[4]{0:T(128)S(1)}, u32[]{:S(2)}) copy-start(s32[4]{0:T(128)S(1)} %get-tuple-element.154) | copy-start | bytes 52
  24.3 95.2 %copy-start.25 = (s32[4]{0:T(128)}, s32[4]{0:T(128)S(1)}, u32[]{:S(2)}) copy-start(s32[4]{0:T(128)S(1)} %get-tuple-element.153) | copy-start | bytes 52
  24.3 99.0 %copy-start.19 = (s32[4]{0:T(128)}, s32[4]{0:T(128)S(1)}, u32[]{:S(2)}) copy-start(s32[4]{0:T(128)S(1)} %get-tuple-element.152) | copy-start | bytes 52
  56.3 136.1 %all-to-all-start.1 = ((bf16[128,4,1024]{0,2,1:T(8,128)(2,1)}), bf16[128,4,1024]{0,2,1:T(8,128)(2,1)}, u32[]{:S(2)}, u32[]{:S(2)}) async-start(bf16[128,4,1024]{0,2,1:T(8,128)(2,1)} %bitcast.211), calls=%async_computation.1 | async-start | bytes 2097152 | tf_op jit(solution)/shard_map/all_to_all | solution.py:90
  80.2 1.7 copy-start.1
  83.1 1.9 copy-start.5
  86.0 10.0 %copy-start.4 = (bf16[128,8,2,128]{0,3,2,1:T(8,128)(2,1)S(1)}, bf16[128,8,2,128]{0,3,2,1:T(8,128)(2,1)}, u32[]{:S(2)}) copy-start(bf16[128,8,2,128]{0,3,2,1:T(8,128)(2,1)} %get-tuple-element.140) | copy-start | bytes 1572868
  86.0 43.1 %collective-permute-start = (bf16[128,2048]{1,0:T(8,128)(2,1)}, bf16[128,2048]{1,0:T(8,128)(2,1)}, u32[]{:S(2)}, u32[]{:S(2)}) collective-permute-start(bf16[128,2048]{1,0:T(8,128)(2,1)} %copy.140), channel_id=1, source_target_pairs={{0,4},{4,8},{8,12},{12,16},{16,20},{20,24},{24,28},{1,5},{5,9},{9,... | collective-permute-start | bytes 1572872 | tf_op jit(solution)/shard_map/ppermute | solution.py:22
  97.0 36.8 %collective-permute-start.1 = (bf16[128,2048]{1,0:T(8,128)(2,1)}, bf16[128,2048]{1,0:T(8,128)(2,1)}, u32[]{:S(2)}, u32[]{:S(2)}) collective-permute-start(bf16[128,2048]{1,0:T(8,128)(2,1)} %copy.141), channel_id=1, source_target_pairs={{4,0},{8,4},{12,8},{16,12},{20,16},{24,20},{28,24},{5,1},{9,5},{13... | collective-permute-start | bytes 1572872 | tf_op jit(solution)/shard_map/ppermute | solution.py:24
  103.0 16.5 %copy-start.3 = (bf16[4,128,2048]{2,0,1:T(4,128)(2,1)}, bf16[4,128,2048]{2,0,1:T(4,128)(2,1)S(1)}, u32[]{:S(2)}) copy-start(bf16[4,128,2048]{2,0,1:T(4,128)(2,1)S(1)} %copy.143) | copy-start | bytes 6291460
  105.6 30.1 %collective-permute-start.3 = (bf16[256,2048]{1,0:T(8,128)(2,1)}, bf16[256,2048]{1,0:T(8,128)(2,1)}, u32[]{:S(2)}, u32[]{:S(2)}) collective-permute-start(bf16[256,2048]{1,0:T(8,128)(2,1)} %bitcast.34), channel_id=1, source_target_pairs={{0,8},{4,12},{8,16},{12,20},{16,24},{20,28},{1,9},{5,13},{9,17},{1... | collective-permute-start | bytes 3145736 | tf_op jit(solution)/shard_map/ppermute | solution.py:34
  115.3 48.3 %collective-permute-start.5 = (bf16[256,2048]{1,0:T(8,128)(2,1)}, bf16[256,2048]{1,0:T(8,128)(2,1)}, u32[]{:S(2)}, u32[]{:S(2)}) collective-permute-start(bf16[256,2048]{1,0:T(8,128)(2,1)} %bitcast.36), channel_id=1, source_target_pairs={{0,4},{4,8},{8,12},{12,16},{16,20},{20,24},{24,28},{1,5},{5,9},{9,... | collective-permute-start | bytes 3145736 | tf_op jit(solution)/shard_map/ppermute | solution.py:34
  120.7 7.0 %slice-start = ((bf16[512,8,3,128]{0,3,2,1:T(8,128)(2,1)}), bf16[512,8,1,128]{0,3,2,1:T(8,128)(2,1)S(1)}, s32[]{:S(2)}) async-start(bf16[512,8,3,128]{0,3,2,1:T(8,128)(2,1)} %copy-done.1), calls=%async_computation.3 | async-start | bytes 2097152 | tf_op jit(solution)/shard_map/slice | solution.py:96
  122.0 43.9 %collective-permute-start.7 = (bf16[256,2048]{1,0:T(8,128)(2,1)}, bf16[256,2048]{1,0:T(8,128)(2,1)}, u32[]{:S(2)}, u32[]{:S(2)}) collective-permute-start(bf16[256,2048]{1,0:T(8,128)(2,1)} %bitcast.38), channel_id=1, source_target_pairs={{4,0},{8,4},{12,8},{16,12},{20,16},{24,20},{28,24},{5,1},{9,5},{13... | collective-permute-start | bytes 3145736 | tf_op jit(solution)/shard_map/ppermute | solution.py:34
  123.3 9.0 %copy-start.2 = (bf16[512,2048]{1,0:T(8,128)(2,1)S(1)}, bf16[512,2048]{1,0:T(8,128)(2,1)}, u32[]{:S(2)}) copy-start(bf16[512,2048]{1,0:T(8,128)(2,1)} %copy.151) | copy-start | bytes 6291460
  129.1 42.2 %collective-permute-start.9 = (bf16[256,2048]{1,0:T(8,128)(2,1)}, bf16[256,2048]{1,0:T(8,128)(2,1)S(1)}, u32[]{:S(2)}, u32[]{:S(2)}) collective-permute-start(bf16[256,2048]{1,0:T(8,128)(2,1)} %bitcast.215), channel_id=1, source_target_pairs={{8,0},{12,4},{16,8},{20,12},{24,16},{28,20},{9,1},{13,5},{17,9},{2... | collective-permute-start | bytes 3145736 | tf_op jit(solution)/shard_map/ppermute | solution.py:34
  185.0 7.5 %copy-start.6 = (bf16[4,128,8,128]{1,3,2,0:T(8,128)(2,1)S(1)}, bf16[4,128,8,128]{1,3,2,0:T(8,128)(2,1)}, u32[]{:S(2)}) copy-start(bf16[4,128,8,128]{1,3,2,0:T(8,128)(2,1)} %custom-call.3) | copy-start | bytes 3145732
  335.7 51.0 %copy-start.7 = (bf16[4,128,8,128]{1,3,2,0:T(8,128)(2,1)}, bf16[4,128,8,128]{1,3,2,0:T(8,128)(2,1)S(1)}, u32[]{:S(2)}) copy-start(bf16[4,128,8,128]{1,3,2,0:T(8,128)(2,1)S(1)} %get-tuple-element.72) | copy-start | bytes 3145732
  335.7 51.0 %copy-start.27 = (s32[28]{0:T(128)S(1)}, s32[28]{0:T(128)}, u32[]{:S(2)}) copy-start(s32[28]{0:T(128)} %eq.235) | copy-start | bytes 340
  427.5 167.4 %collective-permute-start.14 = (f32[2,128,2048]{2,0,1:T(2,128)}, f32[2,128,2048]{2,0,1:T(2,128)}, u32[]{:S(2)}, u32[]{:S(2)}) collective-permute-start(f32[2,128,2048]{2,0,1:T(2,128)} %bitcast.52), channel_id=1, source_target_pairs={{0,4},{4,8},{8,12},{12,16},{16,20},{20,24},{24,28},{1,5},{5,9},{9,... | collective-permute-start | bytes 6291464 | tf_op jit(solution)/shard_map/ppermute | solution.py:34
  430.2 171.2 %collective-permute-start.13 = (f32[2,128,2048]{2,0,1:T(2,128)}, f32[2,128,2048]{2,0,1:T(2,128)}, u32[]{:S(2)}, u32[]{:S(2)}) collective-permute-start(f32[2,128,2048]{2,0,1:T(2,128)} %bitcast.50), channel_id=1, source_target_pairs={{4,0},{8,4},{12,8},{16,12},{20,16},{24,20},{28,24},{5,1},{9,5},{13... | collective-permute-start | bytes 6291464 | tf_op jit(solution)/shard_map/ppermute | solution.py:34
  445.6 45.7 %collective-permute-start.10 = (bf16[128,2048]{1,0:T(8,128)(2,1)S(1)}, bf16[128,2048]{1,0:T(8,128)(2,1)S(1)}, u32[]{:S(2)}, u32[]{:S(2)}) collective-permute-start(bf16[128,2048]{1,0:T(8,128)(2,1)S(1)} %convert_element_type.86), channel_id=1, source_target_pairs={{4,0},{8,4},{12,8},{16,12},{20,16},{24,20},{28,24},{5,1},{9,5},{13... | collective-permute-start | bytes 1572872 | tf_op jit(solution)/shard_map/ppermute | solution.py:34
  447.9 123.5 %collective-permute-start.11 = (bf16[128,2048]{1,0:T(8,128)(2,1)}, bf16[128,2048]{1,0:T(8,128)(2,1)}, u32[]{:S(2)}, u32[]{:S(2)}) collective-permute-start(bf16[128,2048]{1,0:T(8,128)(2,1)} %convert_element_type.88), channel_id=1, source_target_pairs={{0,4},{4,8},{8,12},{12,16},{16,20},{20,24},{24,28},{1,5},{5,9},{9,... | collective-permute-start | bytes 1572872 | tf_op jit(solution)/shard_map/ppermute | solution.py:34
  455.4 152.4 %collective-permute-start.12 = (f32[2,128,2048]{2,0,1:T(2,128)}, f32[2,128,2048]{2,0,1:T(2,128)}, u32[]{:S(2)}, u32[]{:S(2)}) collective-permute-start(f32[2,128,2048]{2,0,1:T(2,128)} %bitcast.48), channel_id=1, source_target_pairs={{8,0},{12,4},{16,8},{20,12},{24,16},{28,20},{9,1},{13,5},{17,9},{2... | collective-permute-start | bytes 6291464 | tf_op jit(solution)/shard_map/ppermute | solution.py:34
  491.3 0.8 copy-start.9
  492.1 122.3 %collective-permute-start.15 = (f32[2,128,2048]{2,0,1:T(2,128)}, f32[2,128,2048]{2,0,1:T(2,128)S(1)}, u32[]{:S(2)}, u32[]{:S(2)}) collective-permute-start(f32[2,128,2048]{2,0,1:T(2,128)} %bitcast.214), channel_id=1, source_target_pairs={{0,8},{4,12},{8,16},{12,20},{16,24},{20,28},{1,9},{5,13},{9,17},{1... | collective-permute-start | bytes 6291464 | tf_op jit(solution)/shard_map/ppermute | solution.py:34
  571.4 23.5 %copy-start.18 = (pred[4]{0:T(512)(128)(4,1)S(1)}, pred[4]{0:T(512)(128)(4,1)}, u32[]{:S(2)}) copy-start(pred[4]{0:T(512)(128)(4,1)} %copy-done.17) | copy-start | bytes 16
  571.4 23.5 %copy-start.26 = (s32[4]{0:T(128)S(1)}, s32[4]{0:T(128)}, u32[]{:S(2)}) copy-start(s32[4]{0:T(128)} %copy-done.25) | copy-start | bytes 52
  594.9 6.5 copy-start.16
  594.9 6.5 copy-start.24
  601.4 6.5 copy-start.14
  601.4 6.5 copy-start.22
  607.8 6.6 copy-start
  607.8 6.6 copy-start.12
  607.8 6.6 copy-start.20
  623.2 3.5 copy-start.8
where the time goes:
time: 681 us; the launch traced here: 670 us
  local copies, waits for them, and re-layouts  318 us (47%)
  starting transfers between devices  111 us (16%)
  matrix products  83.9 us (12%)
  waiting for transfers between devices  76.7 us (11%)
  blocking collectives  39.4 us (6%)
  other arithmetic  38.5 us (6%)
    ppermute x14, starting transfers between devices, from_behind(): lax.ppermute(value, axis, [(source, source + steps) for source in range(i...  96.5 us
    reshape x1, local copies, waits for them, and re-layouts, shards(): flat_terms = pair_terms.reshape(slot_total, BLK * pair_width)  51 us
    dynamic_update_slice x4, local copies, waits for them, and re-layouts, shards(): lax.scan(step, carry_zero, (query_blocks, grad_blocks, places, usable))  46.9 us
    ppermute x14, waiting for transfers between devices, from_behind(): lax.ppermute(value, axis, [(source, source + steps) for source in range(i...  44.7 us
    all_to_all x1, blocking collectives, shards(): lax.all_to_all(joined, 'head', split_axis=0, concat_axis=1, tiled=True)  39.4 us
    scatter-add x2, local copies, waits for them, and re-layouts, shards(): own_grads = own_grads.at[target_block].add(arrived)  39.2 us
    all_to_all x1, waiting for transfers between devices, shards(): lax.all_to_all(qkv, 'head', split_axis=1, concat_axis=0, tiled=True)  32 us
    dot_general x4, matrix products, shards(): jnp.einsum('st,sbf->tbf', owner_tables[side_index], arrived, precision=la...  28.1 us
  transfers between devices with their start and end apart: 18, of which 4 were waited for; matrix products, arithmetic and copies ran while one was open for 28% of the time, Pallas kernels for 0%

commit v1 on v0

--- a/solution.py
+++ b/solution.py
@@ -9,6 +9,22 @@
 DRAWN_TARGET_SET = 4
 SPAN = 2
 NAMED_TILE_LIMIT = 2
+
+
+def exchange_in_pairs(x, axis, split, join):
+    ways, here = (lax.axis_size(axis), lax.axis_index(axis))
+    width = x.shape[split] // ways
+    shape = list(x.shape)
+    shape[split] = width
+    height = shape[join]
+    shape[join] = height * ways
+    full = jnp.zeros(shape, x.dtype)
+    for mask in range(ways):
+        part = lax.dynamic_slice_in_dim(x, (here ^ mask) * width, width, axis=split)
+        if mask:
+            part = lax.ppermute(part, axis, [(d, d ^ mask) for d in range(ways)])
+        full = lax.dynamic_update_slice_in_dim(full, part, (here ^ mask) * height, axis=join)
+    return full
 
 
 def extended_2(cells, sides, width):
@@ -86,7 +102,7 @@
 
 def shards(qkv, grad_out, key_lists, live_counts):
     merged, grad_rows = (
-        lax.all_to_all(qkv, "head", split_axis=1, concat_axis=0, tiled=True),
+        exchange_in_pairs(qkv, "head", 1, 0),
         lax.all_to_all(grad_out, "head", split_axis=1, concat_axis=0, tiled=True),
     )
     row_count = merged.shape[0]

time: 681 us -> 658 us (0.966)
  local copies, waits for them, and re-layouts: 318 us -> 303 us
    all_to_all x1 -> x0, waiting for transfers between devices: 32 us -> none  [shards(): lax.all_to_all(qkv, 'head', split_axis=1, concat_axis=0, tiled=True)]
    ppermute x0 -> x3, waiting for transfers between devices: none -> 25.4 us  [exchange_in_pairs(): part = lax.ppermute(part, axis, [(d, d ^ mask) for d in range(ways)])]
    all_to_all x1 -> x0, local copies, waits for them, and re-layouts: 15.6 us -> none  [shards(): lax.all_to_all(qkv, 'head', split_axis=1, concat_axis=0, tiled=True)]
    unnamed x66 -> x71, local copies, waits for them, and re-layouts: 21.7 us -> 22.6 us
  transfers between devices with their start and end apart: 18 -> 20, of which waited for: 4 -> 5; matrix products, arithmetic and copies ran while one was open for 28% -> 27% of each run, Pallas kernels for 0% -> 0%
where the time goes in v1:
time: 658 us; the launch traced here: 647 us
  local copies, waits for them, and re-layouts  303 us (46%)
  starting transfers between devices  109 us (17%)
  matrix products  83.8 us (13%)
  waiting for transfers between devices  70.9 us (11%)
  blocking collectives  39.5 us (6%)
  other arithmetic  38.5 us (6%)
    ppermute x14, starting transfers between devices, from_behind(): lax.ppermute(value, axis, [(source, source + steps) for source in range(i...  96 us
    reshape x1, local copies, waits for them, and re-layouts, shards(): flat_terms = pair_terms.reshape(slot_total, BLK * pair_width)  51 us
    dynamic_update_slice x4, local copies, waits for them, and re-layouts, shards(): lax.scan(step, carry_zero, (query_blocks, grad_blocks, places, usable))  46.9 us
    ppermute x14, waiting for transfers between devices, from_behind(): lax.ppermute(value, axis, [(source, source + steps) for source in range(i...  45.5 us
    all_to_all x1, blocking collectives, shards(): lax.all_to_all(joined, 'head', split_axis=0, concat_axis=1, tiled=True)  39.5 us
    scatter-add x2, local copies, waits for them, and re-layouts, shards(): own_grads = own_grads.at[target_block].add(arrived)  39.4 us
    dot_general x4, matrix products, shards(): jnp.einsum('st,sbf->tbf', owner_tables[side_index], arrived, precision=la...  28 us
    dot_general x1, matrix products, shards(): jnp.dot(owner_hits, flat_terms, precision=lax.Precision.HIGHEST, preferre...  25.8 us
  transfers between devices with their start and end apart: 20, of which 5 were waited for; matrix products, arithmetic and copies ran while one was open for 27% of the time, Pallas kernels for 0%

profile of v1, /device:TPU:0, one launch (start us, length us, event | category | flops | bytes accessed | tf_op | source)
XLA Modules:
  0.0 646.7 jit_solution(19459729218762658)
XLA Ops:
  0.0 4.9 collective-permute-start.11
  5.0 3.4 collective-permute-start.9
  9.7 2.1 constant_dynamic-slice_fusion.2
  15.6 2.3 copy.124
  17.9 4.2 all-to-all-start
  30.9 2.4 collective-permute-done.7
  36.5 25.4 %collective-permute-done.2 = bf16[128,3072]{0,1:T(8,128)(2,1)S(1)} collective-permute-done((bf16[128,3072]{0,1:T(8,128)(2,1)}, bf16[128,3072]{0,1:T(8,128)(2,1)S(1)}, u32[]{:S(2)}, u32[]{:S(2)}) %collective-permute-start.2) | collective-permute-done | bytes 786464 | tf_op jit(solution)/shard_map/ppermute | solution.py:25
  66.8 2.3 slice.139
  70.1 4.4 collective-permute-start.3
  74.5 2.1 reshape.256
  76.6 2.4 copy.122
  81.3 4.6 copy.114
  88.5 6.8 %collective-permute-start.6 = (bf16[256,2048]{1,0:T(8,128)(2,1)}, bf16[256,2048]{1,0:T(8,128)(2,1)}, u32[]{:S(2)}, u32[]{:S(2)}) collective-permute-start(bf16[256,2048]{1,0:T(8,128)(2,1)} %bitcast.33), channel_id=1, source_target_pairs={{0,8},{4,12},{8,16},{12,20},{16,24},{20,28},{1,9},{5,13},{9,17},{1... | collective-permute-start | bytes 3145736 | tf_op jit(solution)/shard_map/ppermute | solution.py:50
  97.9 3.5 collective-permute-start.8
  105.8 3.0 convolution_convert_fusion
  116.6 1.9 constant_dynamic-update-slice_fusion.4
  118.5 2.3 constant_dynamic-update-slice_fusion.3
  120.8 24.4 %collective-permute-done.8 = bf16[256,2048]{1,0:T(8,128)(2,1)} collective-permute-done((bf16[256,2048]{1,0:T(8,128)(2,1)}, bf16[256,2048]{1,0:T(8,128)(2,1)}, u32[]{:S(2)}, u32[]{:S(2)}) %collective-permute-start.8) | collective-permute-done | bytes 1048608 | tf_op jit(solution)/shard_map/ppermute | solution.py:50
  145.2 2.3 constant_dynamic-update-slice_fusion.2
  147.5 2.4 constant_dynamic-update-slice_fusion.1
  149.9 2.8 collective-permute-done.12
  153.7 12.6 %reshape.225 = bf16[14,128,8,2,128]{4,3,2,1,0:T(2,128)(2,1)} reshape(bf16[1792,2048]{1,0:T(8,128)(2,1)} %constant_dynamic-update-slice_fusion) | data formatting | bytes 14680064 | tf_op jit(solution)/shard_map/reshape | solution.py:157
  166.4 7.5 %copy.125 = bf16[14,128,8,2,128]{4,2,3,1,0:T(8,128)(2,1)} copy(bf16[14,128,8,2,128]{4,3,2,1,0:T(2,128)(2,1)} %reshape.225) | data formatting | bytes 14680064 | tf_op jit(solution)/shard_map/while | solution.py:170
  173.8 139.1 %while.14 = (s32[]{:T(128)}, bf16[4,128,8,128]{1,3,2,0:T(8,128)(2,1)S(1)}, f32[4,7,128,8,2,128]{5,4,3,2,1,0:T(2,128)}, s32[4,7]{1,0:T(4,128)S(1)}, bf16[14,128,8...) while((s32[]{:T(128)}, ...), condition=%wide.region_21.22_spmd, body=%wide.region_17.21_spmd.sunk | while | flops 1203894272 | bytes 104907184 | solution.py:170
  173.8 6.1 gather_fusion
  179.9 2.3 fusion.126
  190.2 2.1 convolution_bitcast_fusion.2
  192.9 3.9 maximum_bitcast_fusion.2
  196.8 11.7 %copy_dynamic-update-slice_fusion.2 = f32[4,7,128,8,2,128]{5,4,3,2,1,0:T(2,128)} fusion(f32[4,7,128,8,2,128]{5,4,3,2,1,0:T(2,128)} %get-tuple-element.220, s32[]{:T(128)S(6)} %copy.205, f32[1,7,128,8,2,128]{5,2,1,3,4,0:T(8,128)} %maximum_bitcast_fusion.2), kind=kLoop, calls=%fused_computation.2.clone.1 | loop fusion | bytes 14680068 | tf_op jit(solution)/shard_map/while/body/jit(dynamic_update_index_in_dim)/dynamic_update_slice | solution.py:170
  208.5 6.1 gather_fusion
  214.6 2.3 fusion.126
  224.9 2.1 convolution_bitcast_fusion.2
  227.6 3.9 maximum_bitcast_fusion.2
  231.5 11.8 %copy_dynamic-update-slice_fusion.2 = f32[4,7,128,8,2,128]{5,4,3,2,1,0:T(2,128)} fusion(f32[4,7,128,8,2,128]{5,4,3,2,1,0:T(2,128)} %get-tuple-element.220, s32[]{:T(128)S(6)} %copy.205, f32[1,7,128,8,2,128]{5,2,1,3,4,0:T(8,128)} %maximum_bitcast_fusion.2), kind=kLoop, calls=%fused_computation.2.clone.1 | loop fusion | bytes 14680068 | tf_op jit(solution)/shard_map/while/body/jit(dynamic_update_index_in_dim)/dynamic_update_slice | solution.py:170
  243.3 6.1 gather_fusion
  249.4 2.3 fusion.126
  259.7 2.1 convolution_bitcast_fusion.2
  262.4 3.9 maximum_bitcast_fusion.2
  266.3 11.8 %copy_dynamic-update-slice_fusion.2 = f32[4,7,128,8,2,128]{5,4,3,2,1,0:T(2,128)} fusion(f32[4,7,128,8,2,128]{5,4,3,2,1,0:T(2,128)} %get-tuple-element.220, s32[]{:T(128)S(6)} %copy.205, f32[1,7,128,8,2,128]{5,2,1,3,4,0:T(8,128)} %maximum_bitcast_fusion.2), kind=kLoop, calls=%fused_computation.2.clone.1 | loop fusion | bytes 14680068 | tf_op jit(solution)/shard_map/while/body/jit(dynamic_update_index_in_dim)/dynamic_update_slice | solution.py:170
  278.1 6.1 gather_fusion
  284.1 2.3 fusion.126
  294.4 2.1 convolution_bitcast_fusion.2
  297.1 3.9 maximum_bitcast_fusion.2
  301.1 11.7 %copy_dynamic-update-slice_fusion.2 = f32[4,7,128,8,2,128]{5,4,3,2,1,0:T(2,128)} fusion(f32[4,7,128,8,2,128]{5,4,3,2,1,0:T(2,128)} %get-tuple-element.220, s32[]{:T(128)S(6)} %copy.205, f32[1,7,128,8,2,128]{5,2,1,3,4,0:T(8,128)} %maximum_bitcast_fusion.2), kind=kLoop, calls=%fused_computation.2.clone.1 | loop fusion | bytes 14680068 | tf_op jit(solution)/shard_map/while/body/jit(dynamic_update_index_in_dim)/dynamic_update_slice | solution.py:170
  312.9 51.0 %reshape.227 = f32[28,262144]{1,0:T(8,128)} reshape(f32[4,7,128,8,2,128]{5,4,3,2,1,0:T(2,128)} %get-tuple-element.73) | data formatting | bytes 58720256 | tf_op jit(solution)/shard_map/reshape | solution.py:173
  363.9 25.8 %fusion.84 = (bf16[14,262144]{1,0:T(8,128)(2,1)}, f32[14,262144]{1,0:T(8,128)}) fusion(f32[28,262144]{1,0:T(8,128)} %reshape.227, s32[28]{0:T(128)S(1)} %copy-done.28), kind=kOutput, calls=%fused_computation.160 | convolution fusion | flops 1236795776 | bytes 51380336 | tf_op jit(solution)/shard_map/dot_general | solution.py:178
  389.6 15.1 %fusion.82 = (f32[2,262144]{1,0:T(2,128)}, f32[2,262144]{1,0:T(2,128)}, f32[2,262144]{1,0:T(2,128)}, f32[2,262144]{1,0:T(2,128)}) fusion(f32[14,262144]{1,0:T(8,128)} %get-tuple-element.141), kind=kLoop, calls=%fused_computation.158 | loop fusion | bytes 16777216 | tf_op jit(solution)/shard_map/slice | solution.py:192
  404.7 2.9 collective-permute-start.17
  409.0 13.9 %slice_reduce_fusion = (bf16[262144]{0:T(1024)(128)(2,1)S(1)}, bf16[262144]{0:T(1024)(128)(2,1)S(1)}) fusion(bf16[14,262144]{1,0:T(8,128)(2,1)} %get-tuple-element.140), kind=kLoop, calls=%fused_computation.47 | loop fusion | bytes 2097152 | tf_op jit(solution)/shard_map/slice | solution.py:184
  425.4 7.2 %collective-permute-start.14 = (bf16[128,2048]{1,0:T(8,128)(2,1)}, bf16[128,2048]{1,0:T(8,128)(2,1)}, u32[]{:S(2)}, u32[]{:S(2)}) collective-permute-start(bf16[128,2048]{1,0:T(8,128)(2,1)} %convert_element_type.88), channel_id=1, source_target_pairs={{0,4},{4,8},{8,12},{12,16},{16,20},{20,24},{24,28},{1,5},{5,9},{9,... | collective-permute-start | bytes 1572872 | tf_op jit(solution)/shard_map/ppermute | solution.py:50
  433.9 13.2 %slice_reduce_fusion.2 = f32[262144]{0:T(1024)S(1)} fusion(f32[14,262144]{1,0:T(8,128)} %get-tuple-element.141), kind=kLoop, calls=%fused_computation.50 | loop fusion | bytes 2097152 | tf_op jit(solution)/shard_map/slice.64
  447.1 5.2 slice.140
  452.5 15.9 %collective-permute-done.13 = bf16[128,2048]{1,0:T(8,128)(2,1)S(1)} collective-permute-done((bf16[128,2048]{1,0:T(8,128)(2,1)S(1)}, bf16[128,2048]{1,0:T(8,128)(2,1)S(1)}, u32[]{:S(2)}, u32[]{:S(2)}) %collective-permute-start.13) | collective-permute-done | bytes 524320 | tf_op jit(solution)/shard_map/ppermute | solution.py:50
  469.2 57.7 %collective-permute-start.18 = (f32[2,128,2048]{2,0,1:T(2,128)}, f32[2,128,2048]{2,0,1:T(2,128)S(1)}, u32[]{:S(2)}, u32[]{:S(2)}) collective-permute-start(f32[2,128,2048]{2,0,1:T(2,128)} %bitcast.211), channel_id=1, source_target_pairs={{0,8},{4,12},{8,16},{12,20},{16,24},{20,28},{1,9},{5,13},{9,17},{1... | collective-permute-start | bytes 6291464 | tf_op jit(solution)/shard_map/ppermute | solution.py:50
  528.8 19.9 %scatter-add.6 = f32[4,128,2048]{2,0,1:T(4,128)} dynamic-update-slice(f32[4,128,2048]{2,0,1:T(4,128)} %bitcast.200, f32[1,128,2048]{2,0,1:T(1,128)S(1)} %add.217, s32[]{:T(128)} %constant.147.clone.1, s32[]{:T(128)} %constant.137.clone.1, s32[]{:T(128)} %constant.137.clone.1) | dynamic-update-slice | bytes 2097156 | tf_op jit(solution)/shard_map/scatter-add | solution.py:189
  549.8 2.9 slice_add_fusion
  552.7 19.5 %scatter-add.9 = f32[4,128,2048]{2,0,1:T(4,128)} dynamic-update-slice(f32[4,128,2048]{2,0,1:T(4,128)} %scatter-add.6, f32[1,128,2048]{2,0,1:T(1,128)S(1)} %slice_add_fusion, s32[]{:T(128)} %constant.137.clone.1, s32[]{:T(128)} %constant.137.clone.1, s32[]{:T(128)} %constant.137.clone.1) | dynamic-update-slice | bytes 2097156 | tf_op jit(solution)/shard_map/scatter-add | solution.py:189
  572.2 6.4 fusion.54
  578.7 6.4 fusion.56
  585.1 6.5 %fusion.58 = f32[4,128,2048]{2,0,1:T(4,128)S(1)} fusion(f32[2,128,2048]{2,0,1:T(2,128)} %collective-permute-done.15, pred[4]{0:T(512)(128)(4,1)S(1)} %copy-done.15, s32[4]{0:T(128)S(1)} %copy-done.23), kind=kOutput, calls=%fused_computation.124 | convolution fusion | flops 25165840 | bytes 6291476 | tf_op jit(solution)/shard_map/st,sbf->tbf/dot_general | solution.py:193
  591.7 8.7 %add_convert_fusion = bf16[4,128,2048]{2,0,1:T(4,128)(2,1)} fusion(f32[4,128,2048]{2,0,1:T(4,128)S(1)} %fusion.54, f32[4,128,2048]{2,0,1:T(4,128)S(1)} %fusion.56, f32[4,128,2048]{2,0,1:T(4,128)S(1)} %copy-done, f32[4,128,2048]{2,0,1:T(4,128)S(1)} %fusion.58, f32[2,128,2048]{2,0,1:T(2,128)S(1)} %collective-permute-done.18, pred[4]{0:T(512)(128)(4,1)S(1)} %copy-done.13, ...), kind=kOutput, calls=%fused_computation.41 | convolution fusion | flops 30408720 | bytes 20971540 | tf_op jit(solution)/shard_map/st,sbf->tbf/dot_general | solution.py:193
  600.4 3.5 copy.154
  604.2 39.5 %all_to_all.32 = bf16[4,128,3072]{1,2,0:T(8,128)(2,1)S(1)} all-to-all(bf16[4,128,3072]{1,2,0:T(8,128)(2,1)S(1)} %bitcast.205), channel_id=1, replica_groups=mesh['ctx'=8,'head'=4] {'head'}, dimensions={0} | all-to-all | bytes 6291456 | tf_op jit(solution)/shard_map/all_to_all | solution.py:199
  643.7 2.8 copy.135
  (198 shorter events, 87.1 us)
Async XLA Ops:
  0.0 27.8 %collective-permute-start.11 = (s32[4,4]{1,0:T(4,128)}, s32[4,4]{1,0:T(4,128)S(1)}, u32[]{:S(2)}, u32[]{:S(2)}) collective-permute-start(s32[4,4]{1,0:T(4,128)} %param.12), channel_id=1, source_target_pairs={{0,8},{4,12},{8,16},{12,20},{16,24},{20,28},{1,9},{5,13},{9,17},{1... | collective-permute-start | bytes 200 | tf_op jit(solution)/shard_map/ppermute | solution.py:50
  5.0 24.2 %collective-permute-start.9 = (s32[4,4]{1,0:T(4,128)}, s32[4,4]{1,0:T(4,128)S(1)}, u32[]{:S(2)}, u32[]{:S(2)}) collective-permute-start(s32[4,4]{1,0:T(4,128)} %param.12), channel_id=1, source_target_pairs={{0,4},{4,8},{8,12},{12,16},{16,20},{20,24},{24,28},{1,5},{5,9},{9,... | collective-permute-start | bytes 200 | tf_op jit(solution)/shard_map/ppermute | solution.py:50
  8.4 22.5 %collective-permute-start.5 = (s32[4,4]{1,0:T(4,128)}, s32[4,4]{1,0:T(4,128)S(1)}, u32[]{:S(2)}, u32[]{:S(2)}) collective-permute-start(s32[4,4]{1,0:T(4,128)} %param.12), channel_id=1, source_target_pairs={{8,0},{12,4},{16,8},{20,12},{24,16},{28,20},{9,1},{13,5},{17,9},{2... | collective-permute-start | bytes 200 | tf_op jit(solution)/shard_map/ppermute | solution.py:50
  11.7 10.4 %copy-start.11 = (s32[4,4]{1,0:T(4,128)S(1)}, s32[4,4]{1,0:T(4,128)}, u32[]{:S(2)}) copy-start(s32[4,4]{1,0:T(4,128)} %param.12) | copy-start | bytes 196
  12.9 20.9 %collective-permute-start = (bf16[128,3072]{0,1:T(8,128)(2,1)}, bf16[128,3072]{0,1:T(8,128)(2,1)}, u32[]{:S(2)}, u32[]{:S(2)}) collective-permute-start(bf16[128,3072]{0,1:T(8,128)(2,1)} %copy.162), channel_id=1, source_target_pairs={{0,1},{1,0},{2,3},{3,2},{4,5},{5,4},{6,7},{7,6},{8,9},{9,8},{10,11... | collective-permute-start | bytes 2359304 | tf_op jit(solution)/shard_map/ppermute | solution.py:25
  14.1 11.6 %copy-start.29 = (s32[4]{0:T(128)S(1)}, s32[4]{0:T(128)}, u32[]{:S(2)}) copy-start(s32[4]{0:T(128)} %param.13) | copy-start | bytes 52
  14.1 21.1 %collective-permute-start.1 = (bf16[128,3072]{0,1:T(8,128)(2,1)}, bf16[128,3072]{0,1:T(8,128)(2,1)}, u32[]{:S(2)}, u32[]{:S(2)}) collective-permute-start(bf16[128,3072]{0,1:T(8,128)(2,1)} %copy.163), channel_id=1, source_target_pairs={{0,2},{1,3},{2,0},{3,1},{4,6},{5,7},{6,4},{7,5},{8,10},{9,11},{10,... | collective-permute-start | bytes 2359304 | tf_op jit(solution)/shard_map/ppermute | solution.py:25
  17.9 155.9 %all-to-all-start = ((bf16[128,4,1024]{0,2,1:T(8,128)(2,1)}), bf16[128,4,1024]{0,2,1:T(8,128)(2,1)}, u32[]{:S(2)}, u32[]{:S(2)}) async-start(bf16[128,4,1024]{0,2,1:T(8,128)(2,1)} %bitcast.41), calls=%async_computation | async-start | bytes 2097152 | tf_op jit(solution)/shard_map/all_to_all | solution.py:106
  26.4 1.1 copy-start.3
  27.8 5.5 collective-permute-start.7
  29.1 32.7 %collective-permute-start.2 = (bf16[128,3072]{0,1:T(8,128)(2,1)}, bf16[128,3072]{0,1:T(8,128)(2,1)S(1)}, u32[]{:S(2)}, u32[]{:S(2)}) collective-permute-start(bf16[128,3072]{0,1:T(8,128)(2,1)} %copy.164), channel_id=1, source_target_pairs={{0,3},{1,2},{2,1},{3,0},{4,7},{5,6},{6,5},{7,4},{8,11},{9,10},{10,... | collective-permute-start | bytes 2359304 | tf_op jit(solution)/shard_map/ppermute | solution.py:25
  33.4 52.5 %copy-start.14 = (pred[4]{0:T(512)(128)(4,1)}, pred[4]{0:T(512)(128)(4,1)S(1)}, u32[]{:S(2)}) copy-start(pred[4]{0:T(512)(128)(4,1)S(1)} %get-tuple-element.106) | copy-start | bytes 16
  33.4 61.9 %copy-start.16 = (pred[4]{0:T(512)(128)(4,1)}, pred[4]{0:T(512)(128)(4,1)S(1)}, u32[]{:S(2)}) copy-start(pred[4]{0:T(512)(128)(4,1)S(1)} %get-tuple-element.107) | copy-start | bytes 16
  33.4 68.0 %copy-start.18 = (pred[4]{0:T(512)(128)(4,1)}, pred[4]{0:T(512)(128)(4,1)S(1)}, u32[]{:S(2)}) copy-start(pred[4]{0:T(512)(128)(4,1)S(1)} %get-tuple-element.105) | copy-start | bytes 16
  33.4 72.3 %copy-start.12 = (pred[4]{0:T(512)(128)(4,1)}, pred[4]{0:T(512)(128)(4,1)S(1)}, u32[]{:S(2)}) copy-start(pred[4]{0:T(512)(128)(4,1)S(1)} %get-tuple-element.104) | copy-start | bytes 16
  33.6 52.3 %copy-start.22 = (s32[4]{0:T(128)}, s32[4]{0:T(128)S(1)}, u32[]{:S(2)}) copy-start(s32[4]{0:T(128)S(1)} %get-tuple-element.145) | copy-start | bytes 52
  33.6 61.7 %copy-start.24 = (s32[4]{0:T(128)}, s32[4]{0:T(128)S(1)}, u32[]{:S(2)}) copy-start(s32[4]{0:T(128)S(1)} %get-tuple-element.144) | copy-start | bytes 52
  33.8 67.6 %copy-start.26 = (s32[4]{0:T(128)}, s32[4]{0:T(128)S(1)}, u32[]{:S(2)}) copy-start(s32[4]{0:T(128)S(1)} %get-tuple-element.143) | copy-start | bytes 52
  33.8 72.0 %copy-start.20 = (s32[4]{0:T(128)}, s32[4]{0:T(128)S(1)}, u32[]{:S(2)}) copy-start(s32[4]{0:T(128)S(1)} %get-tuple-element.142) | copy-start | bytes 52
  62.1 1.7 copy-start.1
  65.0 4.1 copy-start.6
  70.1 8.9 %copy-start.5 = (bf16[128,8,2,128]{0,3,2,1:T(8,128)(2,1)S(1)}, bf16[128,8,2,128]{0,3,2,1:T(8,128)(2,1)}, u32[]{:S(2)}) copy-start(bf16[128,8,2,128]{0,3,2,1:T(8,128)(2,1)} %get-tuple-element.132) | copy-start | bytes 1572868
  70.1 41.8 %collective-permute-start.3 = (bf16[128,2048]{1,0:T(8,128)(2,1)}, bf16[128,2048]{1,0:T(8,128)(2,1)}, u32[]{:S(2)}, u32[]{:S(2)}) collective-permute-start(bf16[128,2048]{1,0:T(8,128)(2,1)} %copy.111), channel_id=1, source_target_pairs={{0,4},{4,8},{8,12},{12,16},{16,20},{20,24},{24,28},{1,5},{5,9},{9,... | collective-permute-start | bytes 1572872 | tf_op jit(solution)/shard_map/ppermute | solution.py:38
  80.0 36.6 %collective-permute-start.4 = (bf16[128,2048]{1,0:T(8,128)(2,1)}, bf16[128,2048]{1,0:T(8,128)(2,1)}, u32[]{:S(2)}, u32[]{:S(2)}) collective-permute-start(bf16[128,2048]{1,0:T(8,128)(2,1)} %copy.112), channel_id=1, source_target_pairs={{4,0},{8,4},{12,8},{16,12},{20,16},{24,20},{28,24},{5,1},{9,5},{13... | collective-permute-start | bytes 1572872 | tf_op jit(solution)/shard_map/ppermute | solution.py:40
  85.9 15.5 %copy-start.4 = (bf16[4,128,2048]{2,0,1:T(4,128)(2,1)}, bf16[4,128,2048]{2,0,1:T(4,128)(2,1)S(1)}, u32[]{:S(2)}) copy-start(bf16[4,128,2048]{2,0,1:T(4,128)(2,1)S(1)} %copy.114) | copy-start | bytes 6291460
  88.5 30.0 %collective-permute-start.6 = (bf16[256,2048]{1,0:T(8,128)(2,1)}, bf16[256,2048]{1,0:T(8,128)(2,1)}, u32[]{:S(2)}, u32[]{:S(2)}) collective-permute-start(bf16[256,2048]{1,0:T(8,128)(2,1)} %bitcast.33), channel_id=1, source_target_pairs={{0,8},{4,12},{8,16},{12,20},{16,24},{20,28},{1,9},{5,13},{9,17},{1... | collective-permute-start | bytes 3145736 | tf_op jit(solution)/shard_map/ppermute | solution.py:50
  97.9 47.4 %collective-permute-start.8 = (bf16[256,2048]{1,0:T(8,128)(2,1)}, bf16[256,2048]{1,0:T(8,128)(2,1)}, u32[]{:S(2)}, u32[]{:S(2)}) collective-permute-start(bf16[256,2048]{1,0:T(8,128)(2,1)} %bitcast.35), channel_id=1, source_target_pairs={{0,4},{4,8},{8,12},{12,16},{16,20},{20,24},{24,28},{1,5},{5,9},{9,... | collective-permute-start | bytes 3145736 | tf_op jit(solution)/shard_map/ppermute | solution.py:50
  104.0 43.5 %collective-permute-start.10 = (bf16[256,2048]{1,0:T(8,128)(2,1)}, bf16[256,2048]{1,0:T(8,128)(2,1)}, u32[]{:S(2)}, u32[]{:S(2)}) collective-permute-start(bf16[256,2048]{1,0:T(8,128)(2,1)} %bitcast.37), channel_id=1, source_target_pairs={{4,0},{8,4},{12,8},{16,12},{20,16},{24,20},{28,24},{5,1},{9,5},{13... | collective-permute-start | bytes 3145736 | tf_op jit(solution)/shard_map/ppermute | solution.py:50
  105.8 9.3 %copy-start.2 = (bf16[512,2048]{1,0:T(8,128)(2,1)S(1)}, bf16[512,2048]{1,0:T(8,128)(2,1)}, u32[]{:S(2)}) copy-start(bf16[512,2048]{1,0:T(8,128)(2,1)} %copy.122) | copy-start | bytes 6291460
  111.9 40.8 %collective-permute-start.12 = (bf16[256,2048]{1,0:T(8,128)(2,1)}, bf16[256,2048]{1,0:T(8,128)(2,1)S(1)}, u32[]{:S(2)}, u32[]{:S(2)}) collective-permute-start(bf16[256,2048]{1,0:T(8,128)(2,1)} %bitcast.212), channel_id=1, source_target_pairs={{8,0},{12,4},{16,8},{20,12},{24,16},{28,20},{9,1},{13,5},{17,9},{2... | collective-permute-start | bytes 3145736 | tf_op jit(solution)/shard_map/ppermute | solution.py:50
  166.3 7.5 %copy-start.7 = (bf16[4,128,8,128]{1,3,2,0:T(8,128)(2,1)S(1)}, bf16[4,128,8,128]{1,3,2,0:T(8,128)(2,1)}, u32[]{:S(2)}) copy-start(bf16[4,128,8,128]{1,3,2,0:T(8,128)(2,1)} %custom-call.3) | copy-start | bytes 3145732
  312.9 51.0 %copy-start.8 = (bf16[4,128,8,128]{1,3,2,0:T(8,128)(2,1)}, bf16[4,128,8,128]{1,3,2,0:T(8,128)(2,1)S(1)}, u32[]{:S(2)}) copy-start(bf16[4,128,8,128]{1,3,2,0:T(8,128)(2,1)S(1)} %get-tuple-element.72) | copy-start | bytes 3145732
  312.9 51.0 %copy-start.28 = (s32[28]{0:T(128)S(1)}, s32[28]{0:T(128)}, u32[]{:S(2)}) copy-start(s32[28]{0:T(128)} %eq.235) | copy-start | bytes 340
  404.7 167.5 %collective-permute-start.17 = (f32[2,128,2048]{2,0,1:T(2,128)}, f32[2,128,2048]{2,0,1:T(2,128)}, u32[]{:S(2)}, u32[]{:S(2)}) collective-permute-start(f32[2,128,2048]{2,0,1:T(2,128)} %bitcast.51), channel_id=1, source_target_pairs={{0,4},{4,8},{8,12},{12,16},{16,20},{20,24},{24,28},{1,5},{5,9},{9,... | collective-permute-start | bytes 6291464 | tf_op jit(solution)/shard_map/ppermute | solution.py:50
  407.7 171.0 %collective-permute-start.16 = (f32[2,128,2048]{2,0,1:T(2,128)}, f32[2,128,2048]{2,0,1:T(2,128)}, u32[]{:S(2)}, u32[]{:S(2)}) collective-permute-start(f32[2,128,2048]{2,0,1:T(2,128)} %bitcast.49), channel_id=1, source_target_pairs={{4,0},{8,4},{12,8},{16,12},{20,16},{24,20},{28,24},{5,1},{9,5},{13... | collective-permute-start | bytes 6291464 | tf_op jit(solution)/shard_map/ppermute | solution.py:50
  423.1 45.3 %collective-permute-start.13 = (bf16[128,2048]{1,0:T(8,128)(2,1)S(1)}, bf16[128,2048]{1,0:T(8,128)(2,1)S(1)}, u32[]{:S(2)}, u32[]{:S(2)}) collective-permute-start(bf16[128,2048]{1,0:T(8,128)(2,1)S(1)} %convert_element_type.86), channel_id=1, source_target_pairs={{4,0},{8,4},{12,8},{16,12},{20,16},{24,20},{28,24},{5,1},{9,5},{13... | collective-permute-start | bytes 1572872 | tf_op jit(solution)/shard_map/ppermute | solution.py:50
  425.4 123.3 %collective-permute-start.14 = (bf16[128,2048]{1,0:T(8,128)(2,1)}, bf16[128,2048]{1,0:T(8,128)(2,1)}, u32[]{:S(2)}, u32[]{:S(2)}) collective-permute-start(bf16[128,2048]{1,0:T(8,128)(2,1)} %convert_element_type.88), channel_id=1, source_target_pairs={{0,4},{4,8},{8,12},{12,16},{16,20},{20,24},{24,28},{1,5},{5,9},{9,... | collective-permute-start | bytes 1572872 | tf_op jit(solution)/shard_map/ppermute | solution.py:50
  432.6 152.5 %collective-permute-start.15 = (f32[2,128,2048]{2,0,1:T(2,128)}, f32[2,128,2048]{2,0,1:T(2,128)}, u32[]{:S(2)}, u32[]{:S(2)}) collective-permute-start(f32[2,128,2048]{2,0,1:T(2,128)} %bitcast.47), channel_id=1, source_target_pairs={{8,0},{12,4},{16,8},{20,12},{24,16},{28,20},{9,1},{13,5},{17,9},{2... | collective-permute-start | bytes 6291464 | tf_op jit(solution)/shard_map/ppermute | solution.py:50
  468.4 0.8 copy-start.10
  469.2 122.5 %collective-permute-start.18 = (f32[2,128,2048]{2,0,1:T(2,128)}, f32[2,128,2048]{2,0,1:T(2,128)S(1)}, u32[]{:S(2)}, u32[]{:S(2)}) collective-permute-start(f32[2,128,2048]{2,0,1:T(2,128)} %bitcast.211), channel_id=1, source_target_pairs={{0,8},{4,12},{8,16},{12,20},{16,24},{20,28},{1,9},{5,13},{9,17},{1... | collective-permute-start | bytes 6291464 | tf_op jit(solution)/shard_map/ppermute | solution.py:50
  548.7 23.5 %copy-start.19 = (pred[4]{0:T(512)(128)(4,1)S(1)}, pred[4]{0:T(512)(128)(4,1)}, u32[]{:S(2)}) copy-start(pred[4]{0:T(512)(128)(4,1)} %copy-done.18) | copy-start | bytes 16
  548.7 23.5 %copy-start.27 = (s32[4]{0:T(128)S(1)}, s32[4]{0:T(128)}, u32[]{:S(2)}) copy-start(s32[4]{0:T(128)} %copy-done.26) | copy-start | bytes 52
  572.2 6.5 copy-start.17
  572.2 6.5 copy-start.25
  578.6 6.5 %copy-start.15 = (pred[4]{0:T(512)(128)(4,1)S(1)}, pred[4]{0:T(512)(128)(4,1)}, u32[]{:S(2)}) copy-start(pred[4]{0:T(512)(128)(4,1)} %copy-done.14) | copy-start | bytes 16
  578.6 6.5 %copy-start.23 = (s32[4]{0:T(128)S(1)}, s32[4]{0:T(128)}, u32[]{:S(2)}) copy-start(s32[4]{0:T(128)} %copy-done.22) | copy-start | bytes 52
  585.1 6.6 %copy-start = (f32[4,128,2048]{2,0,1:T(4,128)S(1)}, f32[4,128,2048]{2,0,1:T(4,128)}, u32[]{:S(2)}) copy-start(f32[4,128,2048]{2,0,1:T(4,128)} %scatter-add.9) | copy-start | bytes 12582916
  585.1 6.6 %copy-start.13 = (pred[4]{0:T(512)(128)(4,1)S(1)}, pred[4]{0:T(512)(128)(4,1)}, u32[]{:S(2)}) copy-start(pred[4]{0:T(512)(128)(4,1)} %copy-done.12) | copy-start | bytes 16
  585.1 6.6 %copy-start.21 = (s32[4]{0:T(128)S(1)}, s32[4]{0:T(128)}, u32[]{:S(2)}) copy-start(s32[4]{0:T(128)} %copy-done.20) | copy-start | bytes 52
  600.4 3.5 copy-start.9
